TPU v7x, 32 devices: a whole 2x2x4 slice. The times are simulated.
32 devices in a mesh: island: 2 (over x), row: 4 (over y, core), col: 4 (over z).
Axes of the slice: x: 2, y: 2, z: 4, core: 2. Of those that a mesh axis runs over, the one named last changes fastest.
Arguments:
- deltas: float32 [2, 4096, 8192], P('island', 'row', 'col'), may hold values from -0.13258252 to 0.13258252
- left_stat: float32 [4096, 4096], P(('island', 'col'), 'row'), may hold values from -1.5 to 1.5
- right_stat: float32 [8192, 8192], P(('island', 'row'), 'col'), may hold values from -1.5 to 1.5
Outputs:
- left_new: float32 [4096, 4096], P(('island', 'col'), 'row')
- right_new: float32 [8192, 8192], P(('island', 'row'), 'col')
All inputs are finite; a program needn't handle non-finite values.
Results may differ from a plain program's by a relative error of at most 0.00037.
Values may be sent and summed in bfloat16 or wider, within the bound.
A program may use at most 128 MiB of HBM per device.

v0:
```python
import jax
import jax.numpy as jnp
from jax import lax
from jax.sharding import PartitionSpec as P

M = 4096
N = 8192


def broadcast(value, axis, source):
    kept = jnp.where(lax.axis_index(axis) == source, value, 0).astype(value.dtype)
    return lax.psum(kept, axis)


def local(deltas, left_stat, right_stat):
    islands = lax.axis_size("island")
    row_count = lax.axis_size("row")
    island = lax.axis_index("island")
    local_delta = deltas[0]
    shares = lax.psum_scatter(local_delta, "island", scatter_dimension=0, tiled=True)
    rounded = (shares / islands).astype(jnp.bfloat16)
    panel = lax.all_gather(rounded, "island", axis=0, tiled=True)
    rows_local = panel.shape[0]
    rows_island = M // islands
    row_pieces = max(1, row_count // islands)
    row_extent = min(rows_island, rows_local)
    blocks = []
    for number in range(row_pieces):
        start_row = island * rows_island + number * row_extent
        source = start_row // rows_local
        blocks.append(broadcast(panel, "row", source))
    left_block = jnp.concatenate(blocks, axis=0)
    left_tile = lax.dot_general(
        left_block, panel, (((1,), (1,)), ((), ())), preferred_element_type=jnp.float32
    )
    left_shares = lax.psum_scatter(left_tile, "col", scatter_dimension=0, tiled=True)
    left_new = left_stat + left_shares
    cols_island = N // islands
    whole_rows = lax.all_gather(panel, "col", axis=1, tiled=True)
    right_block = lax.dynamic_slice_in_dim(whole_rows, island * cols_island, cols_island, 1)
    right_tile = lax.dot_general(
        right_block, panel, (((0,), (0,)), ((), ())), preferred_element_type=jnp.float32
    )
    right_shares = lax.psum_scatter(right_tile, "row", scatter_dimension=0, tiled=True)
    right_new = right_stat + right_shares
    return (left_new, right_new)


def solution(mesh):
    in_specs = (P("island", "row", "col"), P(("island", "col"), "row"), P(("island", "row"), "col"))
    out_specs = (P(("island", "col"), "row"), P(("island", "row"), "col"))
    return jax.shard_map(local, mesh=mesh, in_specs=in_specs, out_specs=out_specs, check_vma=False)
```

profile of v0, /device:TPU:0, one launch (start us, length us, event | category | flops | bytes accessed | tf_op | source)
XLA Modules:
  0.0 1020.4 jit_solution(15273571212736628576)
XLA Ops:
  7.2 0.0 reduce-scatter.4.cloned.1.call-start
  7.2 0.7 reduce-scatter.4.cloned.1.call-update
  7.9 0.0 all-gather.3.cloned.1.call-start
  7.9 104.4 %reduce-scatter.4.cloned.1.call-done = f32[512,2048]{1,0:T(8,128)} async-done(((f32[1024,2048]{1,0:T(8,128)}), f32[512,2048]{1,0:T(8,128)}) %reduce-scatter.4.cloned.1.call-update) | async-done | bytes 4194320 | tf_op jit(solution)/shard_map/reduce_scatter | solution.py:20
  112.3 4.0 multiply_convert_fusion
  116.3 0.0 all-gather.3.cloned.1.call-update
  116.4 0.0 all-reduce.3.cloned.1.call-start
  116.4 56.8 %all-gather.3.cloned.1.call-done = bf16[1024,2048]{1,0:T(8,128)(2,1)} async-done(((bf16[512,2048]{1,0:T(8,128)(2,1)}), bf16[1024,2048]{1,0:T(8,128)(2,1)}) %all-gather.3.cloned.1.call-update) | async-done | bytes 4194320 | tf_op jit(solution)/shard_map/all_gather | solution.py:22
  173.2 6.1 broadcast_select_fusion.1
  179.3 0.0 all-reduce.3.cloned.1.call-update
  179.4 0.0 all-gather.5.cloned.1.call-start
  179.4 0.5 all-gather.5.cloned.1.call-update
  179.9 0.0 reduce-scatter.6.cloned.1.call-start
  180.0 152.4 %all-reduce.3.cloned.1.call-done = (bf16[1024,2048]{1,0:T(8,128)(2,1)}, bf16[1024,2048]{1,0:T(8,128)(2,1)}) async-done(((bf16[1024,2048]{1,0:T(8,128)(2,1)}, bf16[1024,2048]{1,0:T(8,128)(2,1)}), (bf16[1024,2048]{1,0:T(8,128)(2,1)}, bf16[1024,2048]{1,0:T(8,128)(2,1)})) %all-reduce.3.cloned.1.call-update) | async-done | bytes 8388624 | tf_op jit(solution)/shard_map/psum | solution.py:12
  332.4 15.2 %fusion = f32[2048,1024]{1,0:T(8,128)} fusion(bf16[1024,2048]{1,0:T(8,128)(2,1)} %all-gather.3.cloned.1.call-done, bf16[1024,2048]{1,0:T(8,128)(2,1)} %get-tuple-element.2, bf16[1024,2048]{1,0:T(8,128)(2,1)} %get-tuple-element.3), kind=kOutput, calls=%fused_computation | convolution fusion | flops 8606711808 | bytes 20971520 | tf_op jit(solution)/shard_map/dot_general | solution.py:33
  347.6 0.0 reduce-scatter.6.cloned.1.call-update
  347.6 0.2 reduce-scatter.8.cloned.1.call-start
  347.9 272.9 %all-gather.5.cloned.1.call-done = bf16[1024,8192]{1,0:T(8,128)(2,1)} async-done(((bf16[1024,2048]{1,0:T(8,128)(2,1)}), bf16[1024,8192]{1,0:T(8,128)(2,1)}) %all-gather.5.cloned.1.call-update) | async-done | bytes 16777232 | tf_op jit(solution)/shard_map/all_gather | solution.py:39
  620.7 25.6 %fusion.4 = f32[4096,2048]{1,0:T(8,128)} fusion(bf16[1024,2048]{1,0:T(8,128)(2,1)} %all-gather.3.cloned.1.call-done, bf16[1024,8192]{1,0:T(8,128)(2,1)} %all-gather.5.cloned.1.call-done, s32[]{:T(128)S(6)} %select_n.31), kind=kOutput, calls=%fused_computation.4 | convolution fusion | flops 17179869184 | bytes 46137348 | tf_op jit(solution)/shard_map/dot_general | solution.py:41
  646.3 0.0 copy-start
  646.3 0.0 reduce-scatter.8.cloned.1.call-update
  646.3 120.0 %reduce-scatter.6.cloned.1.call-done = f32[512,1024]{1,0:T(8,128)} async-done(((f32[2048,1024]{1,0:T(8,128)}), f32[512,1024]{1,0:T(8,128)}) %reduce-scatter.6.cloned.1.call-update) | async-done | bytes 2097168 | tf_op jit(solution)/shard_map/reduce_scatter | solution.py:36
  766.3 0.0 copy-done
  766.3 3.3 add.25
  769.6 232.1 %reduce-scatter.8.cloned.1.call-done = f32[1024,2048]{1,0:T(8,128)} async-done(((f32[4096,2048]{1,0:T(8,128)}), f32[1024,2048]{1,0:T(8,128)}) %reduce-scatter.8.cloned.1.call-update) | async-done | bytes 8388624 | tf_op jit(solution)/shard_map/reduce_scatter | solution.py:44
  1001.7 11.9 %add.27 = f32[1024,2048]{1,0:T(8,128)} add(f32[1024,2048]{1,0:T(8,128)} %param.5, f32[1024,2048]{1,0:T(8,128)} %reduce-scatter.8.cloned.1.call-done) | non-fusion elementwise | flops 2097152 | bytes 25165824 | tf_op jit(solution)/shard_map/add | solution.py:45
Async XLA Ops:
  7.2 105.2 %reduce-scatter.4.cloned.1.call-start = ((), (), s32[]{:S(2)}) async-start(), calls=%async_computation.3 | async-start | bytes 12582912 | tf_op jit(solution)/shard_map/reduce_scatter | solution.py:20
  7.9 165.4 %all-gather.3.cloned.1.call-start = ((), (), s32[]{:S(2)}) async-start(), calls=%async_computation.4 | async-start | bytes 6291456 | tf_op jit(solution)/shard_map/all_gather | solution.py:22
  116.4 216.0 %all-reduce.3.cloned.1.call-start = ((), (), s32[]{:S(2)}) async-start(), calls=%async_computation.8 | async-start | bytes 16777216 | tf_op jit(solution)/shard_map/psum | solution.py:12
  179.4 441.4 %all-gather.5.cloned.1.call-start = ((), (), s32[]{:S(2)}) async-start(), calls=%async_computation.6 | async-start | bytes 20971520 | tf_op jit(solution)/shard_map/all_gather | solution.py:39
  179.9 586.4 %reduce-scatter.6.cloned.1.call-start = ((), (), s32[]{:S(2)}) async-start(), calls=%async_computation.5 | async-start | bytes 10485760 | tf_op jit(solution)/shard_map/reduce_scatter | solution.py:36
  347.6 654.1 %reduce-scatter.8.cloned.1.call-start = ((), (), s32[]{:S(2)}) async-start(), calls=%async_computation.7 | async-start | bytes 41943040 | tf_op jit(solution)/shard_map/reduce_scatter | solution.py:44
  646.3 120.1 %copy-start = (f32[512,1024]{1,0:T(8,128)S(1)}, f32[512,1024]{1,0:T(8,128)}, u32[]{:S(2)}) copy-start(f32[512,1024]{1,0:T(8,128)} %param.4) | copy-start | bytes 6291460
Sparse Core Ops, SparseCore 0:
  10.3 102.0 reduce-scatter.3
  116.5 56.7 all-gather.2
  179.5 152.8 all-reduce.2
  333.8 286.8 all-gather.4
  623.5 142.7 reduce-scatter.5
  768.8 232.9 reduce-scatter.7
where the time goes:
time: 1020 us
  waiting for transfers between devices  940 us (92%)
  matrix products  40.8 us (4%)
  other arithmetic  25.2 us (2%)
  between operations  14.1 us (1%)
    all_gather x1, waiting for transfers between devices, local(): whole_rows = lax.all_gather(panel, 'col', axis=1, tiled=True)  273 us
    reduce_scatter x1, waiting for transfers between devices, local(): lax.psum_scatter(right_tile, 'row', scatter_dimension=0, tiled=True)  232 us
    psum x1, waiting for transfers between devices, broadcast(): return lax.psum(kept, axis)  152 us
    reduce_scatter x1, waiting for transfers between devices, local(): lax.psum_scatter(left_tile, 'col', scatter_dimension=0, tiled=True)  120 us
    reduce_scatter x1, waiting for transfers between devices, local(): lax.psum_scatter(local_delta, 'island', scatter_dimension=0, tiled=True)  104 us
    all_gather x1, waiting for transfers between devices, local(): panel = lax.all_gather(rounded, 'island', axis=0, tiled=True)  56.8 us
    dot_general x1, matrix products, local(): lax.dot_general(right_block, panel, (((0,), (0,)), ((), ())), preferred_e...  25.6 us
  transfers between devices with their start and end apart: 6, of which 6 were waited for; matrix products, arithmetic and copies ran while one was open for 4% of the time, Pallas kernels for 0%

commit v1 on v0

--- a/solution.py
+++ b/solution.py
@@ -9,7 +9,7 @@
 
 def broadcast(value, axis, source):
     kept = jnp.where(lax.axis_index(axis) == source, value, 0).astype(value.dtype)
-    return lax.psum(kept, axis)
+    return jnp.sum(lax.all_gather(kept, axis), axis=0)
 
 
 def local(deltas, left_stat, right_stat):

time: 1020 us -> 1080 us (1.059)
  waiting for transfers between devices: 940 us -> 974 us
  other arithmetic: 25.2 us -> 50.9 us
    all_gather x0 -> x2, waiting for transfers between devices: none -> 199 us  [broadcast(): return jnp.sum(lax.all_gather(kept, axis), axis=0)]
    psum x1 -> x0, waiting for transfers between devices: 152 us -> none  [broadcast(): return lax.psum(kept, axis)]
    reduce_sum x0 -> x2, other arithmetic: none -> 25.6 us  [broadcast(): return jnp.sum(lax.all_gather(kept, axis), axis=0)]
    all_gather x1, waiting for transfers between devices: 273 us -> 259 us  [local(): whole_rows = lax.all_gather(panel, 'col', axis=1, tiled=True)]
  transfers between devices with their start and end apart: 6 -> 7, of which waited for: 6 -> 7; matrix products, arithmetic and copies ran while one was open for 4% -> 7% of each run, Pallas kernels for 0% -> 0%
where the time goes in v1:
time: 1080 us
  waiting for transfers between devices  974 us (90%)
  other arithmetic  50.9 us (5%)
  matrix products  41.8 us (4%)
  between operations  14.2 us (1%)
    all_gather x1, waiting for transfers between devices, local(): whole_rows = lax.all_gather(panel, 'col', axis=1, tiled=True)  259 us
    reduce_scatter x1, waiting for transfers between devices, local(): lax.psum_scatter(right_tile, 'row', scatter_dimension=0, tiled=True)  232 us
    all_gather x2, waiting for transfers between devices, broadcast(): return jnp.sum(lax.all_gather(kept, axis), axis=0)  199 us
    reduce_scatter x1, waiting for transfers between devices, local(): lax.psum_scatter(left_tile, 'col', scatter_dimension=0, tiled=True)  120 us
    reduce_scatter x1, waiting for transfers between devices, local(): lax.psum_scatter(local_delta, 'island', scatter_dimension=0, tiled=True)  104 us
    all_gather x1, waiting for transfers between devices, local(): panel = lax.all_gather(rounded, 'island', axis=0, tiled=True)  56.8 us
    reduce_sum x2, other arithmetic, broadcast(): return jnp.sum(lax.all_gather(kept, axis), axis=0)  25.6 us
    dot_general x1, matrix products, local(): lax.dot_general(right_block, panel, (((0,), (0,)), ((), ())), preferred_e...  25.5 us
  transfers between devices with their start and end apart: 7, of which 7 were waited for; matrix products, arithmetic and copies ran while one was open for 7% of the time, Pallas kernels for 0%

profile of v1, /device:TPU:0, one launch (start us, length us, event | category | flops | bytes accessed | tf_op | source)
XLA Modules:
  0.0 1080.8 jit_solution(9421333635214112867)
XLA Ops:
  7.2 0.0 reduce-scatter.4.cloned.1.call-start
  7.2 0.7 reduce-scatter.4.cloned.1.call-update
  7.9 0.0 all-gather.7.cloned.1.call-start
  7.9 104.4 %reduce-scatter.4.cloned.1.call-done = f32[512,2048]{1,0:T(8,128)} async-done(((f32[1024,2048]{1,0:T(8,128)}), f32[512,2048]{1,0:T(8,128)}) %reduce-scatter.4.cloned.1.call-update) | async-done | bytes 4194320 | tf_op jit(solution)/shard_map/reduce_scatter | solution.py:20
  112.3 4.0 multiply_convert_fusion
  116.3 0.0 all-gather.7.cloned.1.call-update
  116.4 0.0 all-gather.11.cloned.1.call-start
  116.4 56.8 %all-gather.7.cloned.1.call-done = bf16[1024,2048]{1,0:T(8,128)(2,1)} async-done(((bf16[512,2048]{1,0:T(8,128)(2,1)}), bf16[1024,2048]{1,0:T(8,128)(2,1)}) %all-gather.7.cloned.1.call-update) | async-done | bytes 4194320 | tf_op jit(solution)/shard_map/all_gather | solution.py:22
  173.2 6.1 broadcast_select_fusion.1
  179.3 0.0 all-gather.11.cloned.1.call-update
  179.3 0.0 all-gather.13.cloned.1.call-start
  179.4 0.5 all-gather.13.cloned.1.call-update
  179.9 0.0 all-gather.9.cloned.1.call-start
  180.0 0.5 all-gather.9.cloned.1.call-update
  180.5 0.0 reduce-scatter.6.cloned.1.call-start
  180.6 104.8 %all-gather.11.cloned.1.call-done = bf16[4096,2048]{1,0:T(8,128)(2,1)} async-done(((bf16[1024,2048]{1,0:T(8,128)(2,1)}), bf16[4096,2048]{1,0:T(8,128)(2,1)}) %all-gather.11.cloned.1.call-update) | async-done | bytes 16777232 | tf_op jit(solution)/shard_map/all_gather | solution.py:12
  285.4 12.8 %reduce_sum.24 = bf16[1024,2048]{1,0:T(8,128)(2,1)} reduce(bf16[4,1024,2048]{2,1,0:T(8,128)(2,1)} %bitcast.5, bf16[]{:T(256)} %constant.46.clone.1), dimensions={0}, to_apply=%region_1.2 | reduce | flops 6291456 | bytes 20971522 | tf_op jit(solution)/shard_map/reduce_sum | solution.py:12
  298.2 94.5 %all-gather.13.cloned.1.call-done = bf16[4096,2048]{1,0:T(8,128)(2,1)} async-done(((bf16[1024,2048]{1,0:T(8,128)(2,1)}), bf16[4096,2048]{1,0:T(8,128)(2,1)}) %all-gather.13.cloned.1.call-update) | async-done | bytes 16777232 | tf_op jit(solution)/shard_map/all_gather | solution.py:12
  392.8 12.8 %reduce_sum.25 = bf16[1024,2048]{1,0:T(8,128)(2,1)} reduce(bf16[4,1024,2048]{2,1,0:T(8,128)(2,1)} %bitcast.6, bf16[]{:T(256)} %constant.46.clone.1), dimensions={0}, to_apply=%region_2.3 | reduce | flops 6291456 | bytes 20971522 | tf_op jit(solution)/shard_map/reduce_sum | solution.py:12
  405.5 16.2 %fusion = f32[2048,1024]{1,0:T(8,128)} fusion(bf16[1024,2048]{1,0:T(8,128)(2,1)} %all-gather.7.cloned.1.call-done, bf16[1024,2048]{1,0:T(8,128)(2,1)} %reduce_sum.25, bf16[1024,2048]{1,0:T(8,128)(2,1)} %reduce_sum.24), kind=kOutput, calls=%fused_computation | convolution fusion | flops 8606711808 | bytes 20971520 | tf_op jit(solution)/shard_map/dot_general | solution.py:33
  421.8 0.0 reduce-scatter.6.cloned.1.call-update
  421.8 0.2 reduce-scatter.8.cloned.1.call-start
  422.0 258.9 %all-gather.9.cloned.1.call-done = bf16[1024,8192]{1,0:T(8,128)(2,1)} async-done(((bf16[1024,2048]{1,0:T(8,128)(2,1)}), bf16[1024,8192]{1,0:T(8,128)(2,1)}) %all-gather.9.cloned.1.call-update) | async-done | bytes 16777232 | tf_op jit(solution)/shard_map/all_gather | solution.py:39
  681.0 25.5 %fusion.4 = f32[4096,2048]{1,0:T(8,128)} fusion(bf16[1024,2048]{1,0:T(8,128)(2,1)} %all-gather.7.cloned.1.call-done, bf16[1024,8192]{1,0:T(8,128)(2,1)} %all-gather.9.cloned.1.call-done, s32[]{:T(128)S(6)} %select_n.31), kind=kOutput, calls=%fused_computation.4 | convolution fusion | flops 17179869184 | bytes 46137348 | tf_op jit(solution)/shard_map/dot_general | solution.py:41
  706.5 0.0 copy-start
  706.5 0.0 reduce-scatter.8.cloned.1.call-update
  706.5 120.0 %reduce-scatter.6.cloned.1.call-done = f32[512,1024]{1,0:T(8,128)} async-done(((f32[2048,1024]{1,0:T(8,128)}), f32[512,1024]{1,0:T(8,128)}) %reduce-scatter.6.cloned.1.call-update) | async-done | bytes 2097168 | tf_op jit(solution)/shard_map/reduce_scatter | solution.py:36
  826.6 0.0 copy-done
  826.6 3.3 add.21
  829.9 232.2 %reduce-scatter.8.cloned.1.call-done = f32[1024,2048]{1,0:T(8,128)} async-done(((f32[4096,2048]{1,0:T(8,128)}), f32[1024,2048]{1,0:T(8,128)}) %reduce-scatter.8.cloned.1.call-update) | async-done | bytes 8388624 | tf_op jit(solution)/shard_map/reduce_scatter | solution.py:44
  1062.1 11.9 %add.23 = f32[1024,2048]{1,0:T(8,128)} add(f32[1024,2048]{1,0:T(8,128)} %param.5, f32[1024,2048]{1,0:T(8,128)} %reduce-scatter.8.cloned.1.call-done) | non-fusion elementwise | flops 2097152 | bytes 25165824 | tf_op jit(solution)/shard_map/add | solution.py:45
Async XLA Ops:
  7.2 105.2 %reduce-scatter.4.cloned.1.call-start = ((), (), s32[]{:S(2)}) async-start(), calls=%async_computation.3 | async-start | bytes 12582912 | tf_op jit(solution)/shard_map/reduce_scatter | solution.py:20
  7.9 165.4 %all-gather.7.cloned.1.call-start = ((), (), s32[]{:S(2)}) async-start(), calls=%async_computation.4 | async-start | bytes 6291456 | tf_op jit(solution)/shard_map/all_gather | solution.py:22
  116.4 169.0 %all-gather.11.cloned.1.call-start = ((), (), s32[]{:S(2)}) async-start(), calls=%async_computation.8 | async-start | bytes 20971520 | tf_op jit(solution)/shard_map/all_gather | solution.py:12
  179.3 213.4 %all-gather.13.cloned.1.call-start = ((), (), s32[]{:S(2)}) async-start(), calls=%async_computation.9 | async-start | bytes 20971520 | tf_op jit(solution)/shard_map/all_gather | solution.py:12
  179.9 501.0 %all-gather.9.cloned.1.call-start = ((), (), s32[]{:S(2)}) async-start(), calls=%async_computation.6 | async-start | bytes 20971520 | tf_op jit(solution)/shard_map/all_gather | solution.py:39
  180.5 646.0 %reduce-scatter.6.cloned.1.call-start = ((), (), s32[]{:S(2)}) async-start(), calls=%async_computation.5 | async-start | bytes 10485760 | tf_op jit(solution)/shard_map/reduce_scatter | solution.py:36
  421.8 640.3 %reduce-scatter.8.cloned.1.call-start = ((), (), s32[]{:S(2)}) async-start(), calls=%async_computation.7 | async-start | bytes 41943040 | tf_op jit(solution)/shard_map/reduce_scatter | solution.py:44
  706.5 120.1 %copy-start = (f32[512,1024]{1,0:T(8,128)S(1)}, f32[512,1024]{1,0:T(8,128)}, u32[]{:S(2)}) copy-start(f32[512,1024]{1,0:T(8,128)} %param.4) | copy-start | bytes 6291460
Sparse Core Ops, SparseCore 0:
  10.3 102.0 reduce-scatter.3
  116.5 56.7 all-gather.6
  179.5 105.8 all-gather.10
  286.8 105.8 all-gather.12
  394.2 286.7 all-gather.8
  683.7 142.7 reduce-scatter.5
  829.1 232.9 reduce-scatter.7
